TPU v7x, 32 devices: a whole 2x2x4 slice. The times are simulated.
32 devices in a mesh: dp: 8 (over y, x, core), fsdp: 4 (over z).
Axes of the slice: x: 2, y: 2, z: 4, core: 2. Of those that a mesh axis runs over, the one named last changes fastest.
Arguments:
- tokens_in: bfloat16 [16384, 768], P(('dp', 'fsdp'))
- image_tokens: bfloat16 [65536, 768], P(('dp', 'fsdp'))
- out_cotangent: bfloat16 [16384, 768], P(('dp', 'fsdp')), may hold values from -6 to 6
- caption_lengths: int32 [256], P(('dp', 'fsdp')), may hold values from 1 to 64, as said below
- attn_params: float32 [4721664], P(('dp', 'fsdp'))
- attn_first: float32 [4721664], P(('dp', 'fsdp'))
- attn_second: float32 [4721664], P(('dp', 'fsdp')), as said below
- attn_average: float32 [4721664], P(('dp', 'fsdp'))
- mlp_params: float32 [4720128], P(('dp', 'fsdp'))
- mlp_first: float32 [4720128], P(('dp', 'fsdp'))
- mlp_second: float32 [4720128], P(('dp', 'fsdp')), as said below
- mlp_average: float32 [4720128], P(('dp', 'fsdp'))
- adam_step: int32 [1], replicated, may hold values from 1 to 4
- learn_rate: float32 [1], replicated, may hold values from 0.05 to 0.1
Outputs:
- block_out: bfloat16 [16384, 768], P(('dp', 'fsdp'))
- input_grad: bfloat16 [16384, 768], P(('dp', 'fsdp'))
- image_grad: bfloat16 [65536, 768], P(('dp', 'fsdp'))
- grad_norm: float32 [1], replicated
- attn_first_new: float32 [4721664], P(('dp', 'fsdp'))
- attn_second_new: float32 [4721664], P(('dp', 'fsdp'))
- attn_params_new: float32 [4721664], P(('dp', 'fsdp'))
- attn_average_new: float32 [4721664], P(('dp', 'fsdp'))
- attn_copy: bfloat16 [4721664], P(('dp', 'fsdp'))
- mlp_first_new: float32 [4720128], P(('dp', 'fsdp'))
- mlp_second_new: float32 [4720128], P(('dp', 'fsdp'))
- mlp_params_new: float32 [4720128], P(('dp', 'fsdp'))
- mlp_average_new: float32 [4720128], P(('dp', 'fsdp'))
- mlp_copy: bfloat16 [4720128], P(('dp', 'fsdp'))
Inputs may be any that keep to these rules, and one draw needn't show every extreme that they name: `caption_lengths`: each device's block of 8 consecutive captions holds at least one caption of length 64. `attn_second`: every entry is positive. `mlp_second`: every entry is positive.
All inputs are finite; a program needn't handle non-finite values.
Results may differ from a plain program's by a relative error of at most 0.023.
Values may be sent and summed in bfloat16 or wider, within the bound.
No kernel may reach another device: no remote copies, remote signals or barrier semaphores. Data moves between devices by JAX's collectives and lax.ppermute only.
A program may use at most 256 MiB of HBM per device.

v0:
```python
import jax
import jax.numpy as jnp
from jax import lax
from jax.sharding import PartitionSpec as P

D = 768
HEADS = 12
HD = 64
FF = 3072
IMG = 256
SEQ = 64


clip_limit = 1.0


def layer_norm(rows, gain_row, bias_row):
    center = rows - jnp.mean(rows, axis=-1, keepdims=True)
    spread = jnp.mean(center * center, axis=-1, keepdims=True)
    return center * lax.rsqrt(spread + 1e-05) * gain_row + bias_row


def gelu_tanh(values):
    return (
        0.5
        * values
        * (1.0 + jnp.tanh(0.7978845608028654 * (values + 0.044715 * values * values * values)))
    )


def norm_back(rows, gain_row, bias_row, d_normed):
    unused, pull = jax.vjp(
        layer_norm, rows, gain_row.astype(jnp.float32), bias_row.astype(jnp.float32)
    )
    return pull(d_normed)


def product(form, left, right):
    return jnp.einsum(form, left, right, preferred_element_type=jnp.float32)


def unpack(attn_full, mlp_full):
    square = attn_full[: 8 * D * D].reshape(D, 8 * D)
    norms_attn = attn_full[8 * D * D :].reshape(4, D)
    w_up = mlp_full[: D * FF].reshape(D, FF)
    w_down = mlp_full[D * FF : 2 * D * FF].reshape(FF, D)
    norms_mlp = mlp_full[2 * D * FF :].reshape(2, D)
    return (
        square[:, : 3 * D],
        square[:, 3 * D : 4 * D],
        square[:, 4 * D : 5 * D],
        square[:, 5 * D : 7 * D],
        square[:, 7 * D :],
        norms_attn,
        w_up,
        w_down,
        norms_mlp,
    )


def scores_of(queries, key_rows, allowed):
    scores = product("cqhe,ckhe->chqk", queries, key_rows) * HD ** (-0.5)
    if allowed is not None:
        scores = jnp.where(allowed[:, None], scores, -1e30)
    return scores


def attend_forward(queries, key_rows, value_rows, allowed):
    scores = scores_of(queries, key_rows, allowed)
    top_score = jnp.max(scores, axis=-1, keepdims=True)
    expo = jnp.exp(scores - top_score)
    total = jnp.sum(expo, axis=-1, keepdims=True)
    chance = (expo / total).astype(jnp.bfloat16)
    mixed = product("chqk,ckhe->cqhe", chance, value_rows)
    return (mixed, top_score + jnp.log(total))


def attend_backward(queries, key_rows, value_rows, allowed, log_total, d_mixed):
    scores = scores_of(queries, key_rows, allowed)
    chance = jnp.exp(scores - log_total)
    d_values = product("chqk,cqhe->ckhe", chance.astype(jnp.bfloat16), d_mixed)
    d_chance = product("cqhe,ckhe->chqk", d_mixed, value_rows)
    d_scores = (chance * (d_chance - jnp.sum(chance * d_chance, axis=-1, keepdims=True))).astype(
        jnp.bfloat16
    )
    d_queries = product("chqk,ckhe->cqhe", d_scores, key_rows) * HD ** (-0.5)
    d_keys = product("chqk,cqhe->ckhe", d_scores, queries) * HD ** (-0.5)
    return (d_queries, d_keys, d_values)


def collect(flat_vec):
    return lax.all_gather(flat_vec.astype(jnp.bfloat16), ("dp", "fsdp"), axis=0, tiled=True)


def collect_again(flat_vec):
    return lax.all_gather(flat_vec.astype(jnp.bfloat16), ("dp", "fsdp"), axis=0, tiled=True)


def reduce_grad(flat_grad):
    outer = lax.axis_size("dp")
    inner = lax.axis_size("fsdp")
    shaped = flat_grad.reshape(outer, inner, flat_grad.shape[0] // (outer * inner))
    swapped = lax.all_to_all(
        shaped.astype(jnp.bfloat16), "dp", split_axis=0, concat_axis=0, tiled=True
    ).astype(shaped.dtype)
    part_sum = jnp.sum(swapped, axis=0)
    summed = lax.psum_scatter(
        part_sum.astype(jnp.bfloat16), "fsdp", scatter_dimension=0, tiled=True
    ).astype(jnp.float32)
    return summed.reshape(-1)


def adamw(params, first, second, average, grad, step_value, rate):
    first_new = 0.9 * first + 0.1 * grad
    second_new = 0.999 * second + 0.001 * grad * grad
    first_hat = first_new / (1.0 - jnp.power(0.9, step_value))
    second_hat = second_new / (1.0 - jnp.power(0.999, step_value))
    params_new = params - rate * (first_hat / (jnp.sqrt(second_hat) + 1e-08) + 0.01 * params)
    average_new = 0.8 * average + 0.2 * params_new
    return (first_new, second_new, params_new, average_new, params_new.astype(jnp.bfloat16))


def shards(
    tokens_in,
    image_tokens,
    out_cotangent,
    caption_lengths,
    attn_params,
    attn_first,
    attn_second,
    attn_average,
    mlp_params,
    mlp_first,
    mlp_second,
    mlp_average,
    adam_step,
    learn_rate,
):
    forward_set = unpack(collect(attn_params), collect(mlp_params))
    w_qkv, w_self, w_crossq, w_crosskv, w_crossout, norms_attn, w_up, w_down, norms_mlp = (
        forward_set
    )
    captions = caption_lengths.shape[0]
    position = jnp.arange(SEQ)
    valid = position[None, :] < caption_lengths[:, None]
    allowed = (position[:, None] >= position[None, :])[None] & valid[:, None, :]
    rows_x = tokens_in.astype(jnp.float32)
    normed_one = layer_norm(rows_x, norms_attn[0], norms_attn[1]).astype(jnp.bfloat16)
    qkv_rows = (
        jnp.dot(normed_one, w_qkv, preferred_element_type=jnp.float32)
        .astype(jnp.bfloat16)
        .reshape(captions, SEQ, 3, HEADS, HD)
    )
    self_mix, self_lse = attend_forward(
        qkv_rows[:, :, 0], qkv_rows[:, :, 1], qkv_rows[:, :, 2], allowed
    )
    self_mix = self_mix.reshape(captions * SEQ, D).astype(jnp.bfloat16)
    hidden_one = rows_x + jnp.dot(self_mix, w_self, preferred_element_type=jnp.float32)
    normed_two = layer_norm(hidden_one, norms_attn[2], norms_attn[3]).astype(jnp.bfloat16)
    cross_query = (
        jnp.dot(normed_two, w_crossq, preferred_element_type=jnp.float32)
        .astype(jnp.bfloat16)
        .reshape(captions, SEQ, HEADS, HD)
    )
    cross_kv = (
        jnp.dot(image_tokens, w_crosskv, preferred_element_type=jnp.float32)
        .astype(jnp.bfloat16)
        .reshape(captions, IMG, 2, HEADS, HD)
    )
    cross_mix, cross_lse = attend_forward(cross_query, cross_kv[:, :, 0], cross_kv[:, :, 1], None)
    cross_mix = cross_mix.reshape(captions * SEQ, D).astype(jnp.bfloat16)
    hidden_two = hidden_one + jnp.dot(cross_mix, w_crossout, preferred_element_type=jnp.float32)
    normed_three = layer_norm(hidden_two, norms_mlp[0], norms_mlp[1]).astype(jnp.bfloat16)
    up_rows = jnp.dot(normed_three, w_up, preferred_element_type=jnp.float32)
    activated = gelu_tanh(up_rows).astype(jnp.bfloat16)
    block_out = (
        hidden_two + jnp.dot(activated, w_down, preferred_element_type=jnp.float32)
    ).astype(jnp.bfloat16)
    backward_set = unpack(collect_again(attn_params), collect_again(mlp_params))
    w_qkv, w_self, w_crossq, w_crosskv, w_crossout, norms_attn, w_up, w_down, norms_mlp = (
        backward_set
    )
    valid_rows = valid.reshape(captions * SEQ, 1)
    d_out = jnp.where(valid_rows, out_cotangent, jnp.zeros((), jnp.bfloat16))
    grad_down = product("tf,td->fd", activated, d_out)
    d_act = product("td,fd->tf", d_out, w_down)
    unused_up, gelu_pull = jax.vjp(gelu_tanh, up_rows)
    d_up = gelu_pull(d_act)[0].astype(jnp.bfloat16)
    grad_up = product("td,tf->df", normed_three, d_up)
    d_normed_three = product("tf,df->td", d_up, w_up)
    d_hidden_two, grad_gain_three, grad_bias_three = norm_back(
        hidden_two, norms_mlp[0], norms_mlp[1], d_normed_three
    )
    d_hidden_two = d_hidden_two + d_out.astype(jnp.float32)
    mlp_grad_full = jnp.concatenate(
        [grad_up.reshape(-1), grad_down.reshape(-1), grad_gain_three, grad_bias_three]
    )
    mlp_grad = reduce_grad(mlp_grad_full)
    d_two_low = d_hidden_two.astype(jnp.bfloat16)
    grad_crossout = product("tf,td->fd", cross_mix, d_two_low)
    d_cross_mix = (
        product("td,fd->tf", d_two_low, w_crossout)
        .astype(jnp.bfloat16)
        .reshape(captions, SEQ, HEADS, HD)
    )
    d_query, d_key, d_value = attend_backward(
        cross_query, cross_kv[:, :, 0], cross_kv[:, :, 1], None, cross_lse, d_cross_mix
    )
    d_cross_query = d_query.astype(jnp.bfloat16).reshape(captions * SEQ, D)
    d_cross_kv = (
        jnp.stack([d_key, d_value], axis=2).astype(jnp.bfloat16).reshape(captions * IMG, 2 * D)
    )
    grad_crossq = product("td,tf->df", normed_two, d_cross_query)
    grad_crosskv = product("td,tf->df", image_tokens, d_cross_kv)
    image_grad = product("tf,df->td", d_cross_kv, w_crosskv).astype(jnp.bfloat16)
    d_normed_two = product("tf,df->td", d_cross_query, w_crossq)
    d_hidden_one, grad_gain_two, grad_bias_two = norm_back(
        hidden_one, norms_attn[2], norms_attn[3], d_normed_two
    )
    d_hidden_one = d_hidden_one + d_hidden_two
    d_one_low = d_hidden_one.astype(jnp.bfloat16)
    grad_self = product("tf,td->fd", self_mix, d_one_low)
    d_self_mix = (
        product("td,fd->tf", d_one_low, w_self)
        .astype(jnp.bfloat16)
        .reshape(captions, SEQ, HEADS, HD)
    )
    d_query, d_key, d_value = attend_backward(
        qkv_rows[:, :, 0], qkv_rows[:, :, 1], qkv_rows[:, :, 2], allowed, self_lse, d_self_mix
    )
    d_qkv = (
        jnp.stack([d_query, d_key, d_value], axis=2)
        .astype(jnp.bfloat16)
        .reshape(captions * SEQ, 3 * D)
    )
    grad_qkv = product("td,tf->df", normed_one, d_qkv)
    d_normed_one = product("tf,df->td", d_qkv, w_qkv)
    d_rows, grad_gain_one, grad_bias_one = norm_back(
        rows_x, norms_attn[0], norms_attn[1], d_normed_one
    )
    input_grad = (d_rows + d_hidden_one).astype(jnp.bfloat16)
    square_grad = jnp.concatenate(
        [grad_qkv, grad_self, grad_crossq, grad_crosskv, grad_crossout], axis=1
    )
    attn_grad_full = jnp.concatenate(
        [square_grad.reshape(-1), grad_gain_one, grad_bias_one, grad_gain_two, grad_bias_two]
    )
    attn_grad = reduce_grad(attn_grad_full)
    local_squares = jnp.sum(attn_grad * attn_grad) + jnp.sum(mlp_grad * mlp_grad)
    grad_norm = jnp.sqrt(lax.psum(local_squares, ("dp", "fsdp")))
    clip = jnp.minimum(1.0, clip_limit / (grad_norm + 1e-06))
    step_value = adam_step[0].astype(jnp.float32)
    rate = learn_rate[0]
    attn_new = adamw(
        attn_params, attn_first, attn_second, attn_average, attn_grad * clip, step_value, rate
    )
    mlp_new = adamw(
        mlp_params, mlp_first, mlp_second, mlp_average, mlp_grad * clip, step_value, rate
    )
    return (
        block_out,
        input_grad,
        image_grad,
        grad_norm.reshape(1),
        attn_new[0],
        attn_new[1],
        attn_new[2],
        attn_new[3],
        attn_new[4],
        mlp_new[0],
        mlp_new[1],
        mlp_new[2],
        mlp_new[3],
        mlp_new[4],
    )


def solution(mesh):
    return jax.shard_map(
        shards,
        mesh=mesh,
        in_specs=(
            P(("dp", "fsdp"), None),
            P(("dp", "fsdp"), None),
            P(("dp", "fsdp"), None),
            P(("dp", "fsdp")),
            P(("dp", "fsdp")),
            P(("dp", "fsdp")),
            P(("dp", "fsdp")),
            P(("dp", "fsdp")),
            P(("dp", "fsdp")),
            P(("dp", "fsdp")),
            P(("dp", "fsdp")),
            P(("dp", "fsdp")),
            P(),
            P(),
        ),
        out_specs=(
            P(("dp", "fsdp"), None),
            P(("dp", "fsdp"), None),
            P(("dp", "fsdp"), None),
            P(),
            P(("dp", "fsdp")),
            P(("dp", "fsdp")),
            P(("dp", "fsdp")),
            P(("dp", "fsdp")),
            P(("dp", "fsdp")),
            P(("dp", "fsdp")),
            P(("dp", "fsdp")),
            P(("dp", "fsdp")),
            P(("dp", "fsdp")),
            P(("dp", "fsdp")),
        ),
        check_vma=False,
    )
```

profile of v0, /device:TPU:0, one launch (start us, length us, event | category | flops | bytes accessed | tf_op | source)
XLA Modules:
  0.0 1181.6 jit_solution(2369423407082137884)
XLA Ops:
  10.3 4.3 broadcast.181
  14.6 5.9 dynamic-update-slice
  20.5 4.2 broadcast.182
  24.7 5.8 dynamic-update-slice.1
  34.9 304.7 %all-reduce.9.cloned.1.call-done = (bf16[4721664]{0:T(1024)(128)(2,1)}, bf16[4720128]{0:T(1024)(128)(2,1)}) async-done(((bf16[4721664]{0:T(1024)(128)(2,1)}, bf16[4720128]{0:T(1024)(128)(2,1)}), (bf16[4721664]{0:T(1024)(128)(2,1)}, bf16[4720128]{0:T(1024)(128)(2,1)})) %all-reduce.9.cloned.1.call-update) | async-done | bytes 18883600
  339.6 9.6 slice.121
  349.9 3.9 fusion.94
  353.8 14.0 %reshape.301 = bf16[768,6144]{1,0:T(8,128)(2,1)} reshape(bf16[4718592]{0:T(1024)(128)(2,1)} %slice.121) | data formatting | bytes 18874368 | tf_op jit(solution)/shard_map/reshape | solution.py:43
  367.8 5.8 convolution_convert_fusion.4
  373.6 4.3 copy.159
  377.9 7.0 reshape.302
  385.0 4.7 fusion.96
  404.3 3.9 convert_element_type.181
  418.8 4.1 copy.187
  423.0 7.0 convolution_convert_fusion
  448.9 4.0 fusion.99
  452.8 9.2 slice.118
  462.1 8.2 reshape.305
  472.2 5.3 fusion.86
  477.6 9.5 fusion.3
  499.9 4.1 copy.188
  504.0 7.5 multiply_reduce_fusion
  511.6 4.6 multiply_convert_fusion.1
  540.8 4.1 copy.183
  563.9 7.0 copy.186
  570.9 7.5 convert_element_type.208
  578.4 6.4 fusion.87
  584.8 4.2 fusion.7
  589.1 5.0 convolution_convert_fusion.1
  594.1 5.1 fusion.31
  599.9 4.6 copy.189
  604.5 5.4 copy.225
  613.9 7.0 fusion.19
  622.8 10.4 copy.226
  633.2 8.6 constant_dynamic-update-slice_fusion
  641.8 9.2 reshape.311
  651.0 3.9 copy.227
  654.9 45.3 %pad_maximum_fusion = bf16[4720128]{0:T(1024)(128)(2,1)} fusion(bf16[768]{0:T(1024)(128)(2,1)S(1)} %get-tuple-element.30, bf16[768]{0:T(1024)(128)(2,1)S(1)} %get-tuple-element.24, bf16[2359296]{0:T(1024)(128)(2,1)S(1)} %copy-done.4, bf16[2359296]{0:T(1024)(128)(2,1)S(1)} %bitcast.150), kind=kLoop, calls=%fused_computation | loop fusion | flops 37761024 | bytes 18880512 | tf_op jit(solution)/shard_map/concatenate | solution.py:195
  700.2 73.0 %while.3 = (u32[]{:T(128)}, bf16[4720128]{0:T(1024)(128)(2,1)}, bf16[8,4,147504]{2,1,0:T(4,128)(2,1)}, u32[]{}, u32[]{}, /*index=5*/u32[]{}, u32[]{}) while((u32[]{:T(128)}, bf16[4720128]{0:T(1024)(128)(2,1)}, bf16[8,4,147504]{2,1,0:T(4,128)(2,1)}, u32[]{}, u32[]{}, /*index=5*/u32[]{}, u32[]{}) %tuple.67), condition=%wide.cond.1, body=%wide.body.1.sunk | while | flops 9 | bytes 7081653
  703.1 3.9 reshape.329
  712.3 3.9 reshape.329
  721.4 3.9 reshape.329
  730.5 3.9 reshape.329
  739.7 3.9 reshape.329
  748.8 3.9 reshape.329
  757.9 3.9 reshape.329
  767.0 3.9 reshape.329
  773.2 5.3 all-to-all-start.1
  786.5 73.0 %while.2 = (u32[]{:T(128)}, bf16[4721664]{0:T(1024)(128)(2,1)}, bf16[8,4,147552]{2,1,0:T(4,128)(2,1)}, u32[]{}, u32[]{}, /*index=5*/u32[]{}, u32[]{}) while((u32[]{:T(128)}, bf16[4721664]{0:T(1024)(128)(2,1)}, bf16[8,4,147552]{2,1,0:T(4,128)(2,1)}, u32[]{}, u32[]{}, /*index=5*/u32[]{}, u32[]{}) %tuple.64), condition=%wide.cond, body=%wide.body.sunk | while | flops 9 | bytes 7083189
  789.5 3.9 reshape.328
  798.6 3.9 reshape.328
  807.7 3.9 reshape.328
  816.8 3.9 reshape.328
  859.5 24.4 %all-to-all-done.1 = bf16[8,4,147504]{2,1,0:T(4,128)(2,1)} async-done(((bf16[8,4,147504]{2,1,0:T(4,128)(2,1)}), bf16[8,4,147504]{2,1,0:T(4,128)(2,1)}, u32[]{:S(2)}, u32[]{:S(2)}) %all-to-all-start.1) | async-done | bytes 9440288 | tf_op jit(solution)/shard_map/all_to_all | solution.py:103
  884.0 5.2 all-to-all-start
  891.2 11.4 reduce_sum.280
  902.6 91.9 %all-to-all-done = bf16[8,4,147552]{2,1,0:T(4,128)(2,1)} async-done(((bf16[8,4,147552]{2,1,0:T(4,128)(2,1)}), bf16[8,4,147552]{2,1,0:T(4,128)(2,1)}, u32[]{:S(2)}, u32[]{:S(2)}) %all-to-all-start) | async-done | bytes 9443360 | tf_op jit(solution)/shard_map/all_to_all | solution.py:103
  994.5 11.4 reduce_sum.273
  1006.0 9.7 add_convert_fusion.1
  1015.6 9.2 convolution_convert_fusion.6
  1024.8 74.2 %all-reduce.11.cloned.1.call-done = (bf16[4,147552]{1,0:T(4,128)(2,1)}, bf16[4,147504]{1,0:T(4,128)(2,1)}) async-done(((bf16[4,147552]{1,0:T(4,128)(2,1)}, bf16[4,147504]{1,0:T(4,128)(2,1)}), (bf16[4,147552]{1,0:T(4,128)(2,1)}, bf16[4,147504]{1,0:T(4,128)(2,1)})) %all-reduce.11.cloned.1.call-update) | async-done | bytes 2360464
  1111.0 39.4 %psum.7 = f32[]{:T(128)} all-reduce(f32[]{:T(128)S(6)} %add.167), channel_id=1, replica_groups=mesh['dp'=8,'fsdp'=4] {'dp','fsdp'}, use_global_device_ids=true, to_apply=%region_30.31 | all-reduce | flops 1 | bytes 8 | tf_op jit(solution)/shard_map/psum | solution.py:250
  1151.1 7.9 multiply_reduce_fusion.10
  1159.0 7.8 multiply_reduce_fusion.9
  (251 shorter events, 242.2 us)
Async XLA Ops:
  7.2 415.8 %copy-start = (bf16[2048,768]{1,0:T(8,128)(2,1)S(1)}, bf16[2048,768]{1,0:T(8,128)(2,1)}, u32[]{:S(2)}) copy-start(bf16[2048,768]{1,0:T(8,128)(2,1)} %param.15) | copy-start | bytes 9437188
  7.2 332.4 %all-reduce.9.cloned.1.call-start = ((), (), s32[]{:S(2)}) async-start(), calls=%async_computation.2 | async-start | bytes 37769216
  339.6 9.6 copy-start.28
  398.4 3.5 copy-start.2
  398.5 2.5 copy-start.29
  410.9 1.1 copy-start.11
  432.7 1.4 copy-start.18
  433.3 3.3 copy-start.20
  433.3 5.5 copy-start.25
  436.6 2.6 copy-start.1
  470.3 7.2 slice-start.2
  472.2 5.4 slice-start.3
  472.2 5.4 copy-start.32
  472.2 14.9 %slice-start.4 = ((s8[4718592]{0:T(1024)(128)(4,1)}), s8[4194304]{0:T(1024)(128)(4,1)S(1)}, s32[]{:S(2)}) async-start(s8[4718592]{0:T(1024)(128)(4,1)} %bitcast.157), calls=%async_computation.8 | async-start | bytes 8388608
  477.6 9.5 copy-start.52
  477.6 9.5 copy-start.9
  477.6 9.5 slice-start.5
  487.1 3.0 copy-start.53
  490.8 1.2 copy-start.16
  511.6 6.3 copy-start.21
  516.2 1.7 copy-start.26
  527.4 3.5 copy-start.12
  530.8 1.4 copy-start.17
  530.8 1.6 copy-start.33
  532.8 1.2 copy-start.6
  544.9 3.5 copy-start.3
  544.9 3.8 copy-start.5
  544.9 4.2 copy-start.30
  550.3 1.4 copy-start.15
  550.3 3.8 slice-start
  551.7 1.7 copy-start.14
  551.7 2.6 slice-start.1
  553.4 1.6 copy-start.8
  555.0 2.7 copy-start.19
  555.0 3.5 copy-start.27
  578.4 6.4 copy-start.24
  578.4 6.4 copy-start.40
  578.4 10.7 slice-start.6
  584.8 4.3 copy-start.34
  584.8 4.3 slice-start.7
  589.1 5.1 copy-start.10
  589.1 5.0 copy-start.54
  594.1 5.1 copy-start.49
  594.1 5.1 copy-start.22
  594.1 5.1 copy-start.23
  604.4 5.4 copy-start.7
  604.4 5.4 copy-start.35
  604.4 7.3 copy-start.43
  609.8 1.9 copy-start.13
  609.8 4.0 copy-start.31
  613.9 7.0 copy-start.36
  613.9 7.0 copy-start.42
  651.0 3.9 copy-start.4
  773.2 110.7 %all-to-all-start.1 = ((bf16[8,4,147504]{2,1,0:T(4,128)(2,1)}), bf16[8,4,147504]{2,1,0:T(4,128)(2,1)}, u32[]{:S(2)}, u32[]{:S(2)}) async-start(bf16[8,4,147504]{2,1,0:T(4,128)(2,1)} %get-tuple-element.23), calls=%async_computation.1 | async-start | bytes 18890752 | tf_op jit(solution)/shard_map/all_to_all | solution.py:103
  884.0 6.6 copy-start.51
  884.0 110.5 %all-to-all-start = ((bf16[8,4,147552]{2,1,0:T(4,128)(2,1)}), bf16[8,4,147552]{2,1,0:T(4,128)(2,1)}, u32[]{:S(2)}, u32[]{:S(2)}) async-start(bf16[8,4,147552]{2,1,0:T(4,128)(2,1)} %get-tuple-element.18), calls=%async_computation | async-start | bytes 18890752 | tf_op jit(solution)/shard_map/all_to_all | solution.py:103
  889.1 209.9 %all-reduce.11.cloned.1.call-start = ((), (), s32[]{:S(2)}) async-start(), calls=%async_computation.3 | async-start | bytes 4722688
  1151.1 18.7 %copy-start.44 = (f32[147552]{0:T(1024)S(1)}, f32[147552]{0:T(1024)}, u32[]{:S(2)}) copy-start(f32[147552]{0:T(1024)} %param.21) | copy-start | bytes 1770628
  1166.9 3.9 copy-start.37
  1166.9 3.9 copy-start.46
  1166.9 3.9 copy-start.47
  1169.8 3.4 copy-start.38
  1169.8 2.3 copy-start.45
  1172.2 1.0 copy-start.39
  (3 other events, 2.1 us)
Sparse Core Ops, SparseCore 0:
  30.7 308.8 all-reduce.8
  1006.1 92.9 all-reduce.10
where the time goes:
time: 1200 us; the launch traced here: 1180 us
  waiting for transfers between devices  495 us (41%)
  local copies, waits for them, and re-layouts  356 us (30%)
  matrix products  134 us (11%)
  other arithmetic  126 us (10%)
  blocking collectives  39.4 us (3%)
  between operations  19.9 us (2%)
    unnamed x4, waiting for transfers between devices  379 us
    unnamed x189, local copies, waits for them, and re-layouts  223 us
    all_to_all x2, waiting for transfers between devices, reduce_grad(): lax.all_to_all(shaped.astype(jnp.bfloat16), 'dp', split_axis=0, concat_ax...  116 us
    dot_general x26, matrix products, product(): return jnp.einsum(form, left, right, preferred_element_type=jnp.float32)  96.3 us
    concatenate x1, other arithmetic, shards(): jnp.concatenate([grad_up.reshape(-1), grad_down.reshape(-1), grad_gain_th...  45.3 us
    psum x1, blocking collectives, shards(): grad_norm = jnp.sqrt(lax.psum(local_squares, ('dp', 'fsdp')))  39.4 us
  transfers between devices with their start and end apart: 4, of which 4 were waited for; matrix products, arithmetic and copies ran while one was open for 10% of the time, Pallas kernels for 0%

commit v1 on v0

--- a/solution.py
+++ b/solution.py
@@ -9,6 +9,8 @@
 FF = 3072
 IMG = 256
 SEQ = 64
+AXES = ("dp", "fsdp")
+NORMS = 6 * D
 
 
 clip_limit = 1.0
@@ -39,23 +41,116 @@
     return jnp.einsum(form, left, right, preferred_element_type=jnp.float32)
 
 
-def unpack(attn_full, mlp_full):
-    square = attn_full[: 8 * D * D].reshape(D, 8 * D)
-    norms_attn = attn_full[8 * D * D :].reshape(4, D)
-    w_up = mlp_full[: D * FF].reshape(D, FF)
-    w_down = mlp_full[D * FF : 2 * D * FF].reshape(FF, D)
-    norms_mlp = mlp_full[2 * D * FF :].reshape(2, D)
+def round_up(count, step):
+    return -(-count // step) * step
+
+
+def device_count():
+    return lax.axis_size(AXES)
+
+
+def own_index():
+    return lax.axis_index(AXES)
+
+
+def next_pairs(count):
+    return [(i, i + 1) for i in range(count - 1)]
+
+
+def prior_pairs(count):
+    return [(i + 1, i) for i in range(count - 1)]
+
+
+def align_shard(flat_vec, tail):
+    count = device_count()
+    step = tail // count
+    size = flat_vec.shape[0] - step
+    low = flat_vec.astype(jnp.bfloat16)
+    ending = low[flat_vec.shape[0] - tail :]
+    before = lax.ppermute(ending, AXES, next_pairs(count))
+    both = jnp.concatenate([before, low])
+    block = lax.dynamic_slice(both, (tail - step * own_index(),), (size,))
+    return block, ending
+
+
+def unalign_shard(block, ending, tail):
+    count = device_count()
+    step = tail // count
+    index = own_index()
+    after = lax.ppermute(block[:tail], AXES, prior_pairs(count))
+    after = jnp.where(index == count - 1, ending, after)
+    both = jnp.concatenate([block, after])
+    return lax.dynamic_slice(both, (step * index,), (block.shape[0] + step,))
+
+
+def gather_weights(attn_params, mlp_params):
+    count = device_count()
+    rows = D // count
+    width = round_up(NORMS // rows, 128)
+    attn_block, attn_end = align_shard(attn_params, 4 * D)
+    mlp_block, mlp_end = align_shard(mlp_params, 2 * D)
+    norms = jnp.concatenate(
+        [attn_end, mlp_end, jnp.zeros((rows * width - NORMS,), jnp.bfloat16)]
+    )
+    attn_rows = jnp.concatenate(
+        [attn_block.reshape(rows, 8 * D), norms.reshape(rows, width)], axis=1
+    )
+    half = count // 2
+    up_rows = D // half
+    as_up = mlp_block.reshape(up_rows, 4, D).swapaxes(0, 1)
+    as_down = mlp_block.reshape(4, up_rows, D)
+    mlp_rows = jnp.where(own_index() < half, as_up, as_down)
+    square = lax.all_gather(attn_rows, AXES, axis=0, tiled=True)
+    stack = lax.all_gather(mlp_rows, AXES, axis=0, tiled=True)
+    stack = stack.reshape(2, half, 4, up_rows, D)
+    w_up = stack[0].swapaxes(1, 2).reshape(D, FF)
+    w_down = stack[1].reshape(FF, D)
+    vectors = square[D - rows :, 8 * D :].reshape(-1)
     return (
         square[:, : 3 * D],
         square[:, 3 * D : 4 * D],
         square[:, 4 * D : 5 * D],
         square[:, 5 * D : 7 * D],
-        square[:, 7 * D :],
-        norms_attn,
+        square[:, 7 * D : 8 * D],
+        vectors[: 4 * D].reshape(4, D),
         w_up,
         w_down,
-        norms_mlp,
-    )
+        vectors[4 * D : 6 * D].reshape(2, D),
+    )
+
+
+def scatter_sum(full):
+    part = lax.psum_scatter(full, "dp", scatter_dimension=0, tiled=True)
+    return lax.psum_scatter(part, "fsdp", scatter_dimension=0, tiled=True)
+
+
+def reduce_mlp(grad_up, grad_down):
+    count = device_count()
+    half = count // 2
+    up_rows = D // half
+    up_part = grad_up.reshape(half, up_rows, 4, D).swapaxes(1, 2).reshape(FF, D)
+    summed = scatter_sum(jnp.concatenate([up_part, grad_down], axis=0))
+    summed = summed.reshape(4, up_rows, D)
+    return jnp.where(
+        own_index() < half, summed.swapaxes(0, 1).reshape(-1), summed.reshape(-1)
+    ).astype(jnp.float32)
+
+
+def reduce_attn(parts, norm_grads):
+    rows = D // device_count()
+    width = round_up(NORMS // rows, 128)
+    norms = jnp.concatenate(
+        [norm_grads.reshape(-1), jnp.zeros((rows * width - NORMS,), jnp.float32)]
+    ).reshape(rows, width)
+    norms = jnp.pad(norms, ((D - rows, 0), (0, 0))).astype(jnp.bfloat16)
+    summed = scatter_sum(jnp.concatenate(list(parts) + [norms], axis=1)).astype(jnp.float32)
+    return summed[:, : 8 * D].reshape(-1), summed[:, 8 * D :].reshape(-1)[:NORMS]
+
+
+def sum_everywhere(value):
+    count = device_count()
+    row = jnp.broadcast_to(value.reshape(1, 1), (count, 128))
+    return jnp.sum(lax.all_to_all(row, AXES, split_axis=0, concat_axis=0, tiled=True)[:, 0])
 
 
 def scores_of(queries, key_rows, allowed):
@@ -86,28 +181,6 @@
     d_queries = product("chqk,ckhe->cqhe", d_scores, key_rows) * HD ** (-0.5)
     d_keys = product("chqk,cqhe->ckhe", d_scores, queries) * HD ** (-0.5)
     return (d_queries, d_keys, d_values)
-
-
-def collect(flat_vec):
-    return lax.all_gather(flat_vec.astype(jnp.bfloat16), ("dp", "fsdp"), axis=0, tiled=True)
-
-
-def collect_again(flat_vec):
-    return lax.all_gather(flat_vec.astype(jnp.bfloat16), ("dp", "fsdp"), axis=0, tiled=True)
-
-
-def reduce_grad(flat_grad):
-    outer = lax.axis_size("dp")
-    inner = lax.axis_size("fsdp")
-    shaped = flat_grad.reshape(outer, inner, flat_grad.shape[0] // (outer * inner))
-    swapped = lax.all_to_all(
-        shaped.astype(jnp.bfloat16), "dp", split_axis=0, concat_axis=0, tiled=True
-    ).astype(shaped.dtype)
-    part_sum = jnp.sum(swapped, axis=0)
-    summed = lax.psum_scatter(
-        part_sum.astype(jnp.bfloat16), "fsdp", scatter_dimension=0, tiled=True
-    ).astype(jnp.float32)
-    return summed.reshape(-1)
 
 
 def adamw(params, first, second, average, grad, step_value, rate):
@@ -136,9 +209,8 @@
     adam_step,
     learn_rate,
 ):
-    forward_set = unpack(collect(attn_params), collect(mlp_params))
     w_qkv, w_self, w_crossq, w_crosskv, w_crossout, norms_attn, w_up, w_down, norms_mlp = (
-        forward_set
+        gather_weights(attn_params, mlp_params)
     )
     captions = caption_lengths.shape[0]
     position = jnp.arange(SEQ)
@@ -176,10 +248,6 @@
     block_out = (
         hidden_two + jnp.dot(activated, w_down, preferred_element_type=jnp.float32)
     ).astype(jnp.bfloat16)
-    backward_set = unpack(collect_again(attn_params), collect_again(mlp_params))
-    w_qkv, w_self, w_crossq, w_crosskv, w_crossout, norms_attn, w_up, w_down, norms_mlp = (
-        backward_set
-    )
     valid_rows = valid.reshape(captions * SEQ, 1)
     d_out = jnp.where(valid_rows, out_cotangent, jnp.zeros((), jnp.bfloat16))
     grad_down = product("tf,td->fd", activated, d_out)
@@ -192,10 +260,7 @@
         hidden_two, norms_mlp[0], norms_mlp[1], d_normed_three
     )
     d_hidden_two = d_hidden_two + d_out.astype(jnp.float32)
-    mlp_grad_full = jnp.concatenate(
-        [grad_up.reshape(-1), grad_down.reshape(-1), grad_gain_three, grad_bias_three]
-    )
-    mlp_grad = reduce_grad(mlp_grad_full)
+    mlp_block = reduce_mlp(grad_up.astype(jnp.bfloat16), grad_down.astype(jnp.bfloat16))
     d_two_low = d_hidden_two.astype(jnp.bfloat16)
     grad_crossout = product("tf,td->fd", cross_mix, d_two_low)
     d_cross_mix = (
@@ -239,15 +304,30 @@
         rows_x, norms_attn[0], norms_attn[1], d_normed_one
     )
     input_grad = (d_rows + d_hidden_one).astype(jnp.bfloat16)
-    square_grad = jnp.concatenate(
-        [grad_qkv, grad_self, grad_crossq, grad_crosskv, grad_crossout], axis=1
-    )
-    attn_grad_full = jnp.concatenate(
-        [square_grad.reshape(-1), grad_gain_one, grad_bias_one, grad_gain_two, grad_bias_two]
-    )
-    attn_grad = reduce_grad(attn_grad_full)
-    local_squares = jnp.sum(attn_grad * attn_grad) + jnp.sum(mlp_grad * mlp_grad)
-    grad_norm = jnp.sqrt(lax.psum(local_squares, ("dp", "fsdp")))
+    attn_block, norm_block = reduce_attn(
+        [
+            grad.astype(jnp.bfloat16)
+            for grad in (grad_qkv, grad_self, grad_crossq, grad_crosskv, grad_crossout)
+        ],
+        jnp.stack(
+            [
+                grad_gain_one,
+                grad_bias_one,
+                grad_gain_two,
+                grad_bias_two,
+                grad_gain_three,
+                grad_bias_three,
+            ]
+        ),
+    )
+    local_squares = (
+        jnp.sum(attn_block * attn_block)
+        + jnp.sum(mlp_block * mlp_block)
+        + jnp.sum(norm_block * norm_block)
+    )
+    grad_norm = jnp.sqrt(sum_everywhere(local_squares))
+    attn_grad = unalign_shard(attn_block, norm_block[: 4 * D], 4 * D)
+    mlp_grad = unalign_shard(mlp_block, norm_block[4 * D :], 2 * D)
     clip = jnp.minimum(1.0, clip_limit / (grad_norm + 1e-06))
     step_value = adam_step[0].astype(jnp.float32)
     rate = learn_rate[0]

time: 1200 us -> 644 us (0.54)
  waiting for transfers between devices: 495 us -> 254 us
  local copies, waits for them, and re-layouts: 356 us -> 148 us
  other arithmetic: 126 us -> 57.1 us
  blocking collectives: 39.4 us -> 0 us
    unnamed x4 -> x6, waiting for transfers between devices: 379 us -> 0.1 us
    unnamed x189 -> x144, local copies, waits for them, and re-layouts: 223 us -> 34.9 us
    all_gather x0 -> x2, waiting for transfers between devices: none -> 143 us  [the longest x1 72.9 us: gather_weights(): square = lax.all_gather(attn_rows, AXES, axis=0, tiled=True)]
    all_to_all x2 -> x1, waiting for transfers between devices: 116 us -> 1.53 us  [sum_everywhere(): lax.all_to_all(row, AXES, split_axis=0, concat_axis=0, tiled=True)[:, 0]]
    reduce_scatter x0 -> x4, waiting for transfers between devices: none -> 103 us  [the longest x2 52.3 us: scatter_sum(): return lax.psum_scatter(part, 'fsdp', scatter_dimension=0, tiled=True)]
    psum x1 -> x0, blocking collectives: 39.4 us -> none  [shards(): grad_norm = jnp.sqrt(lax.psum(local_squares, ('dp', 'fsdp')))]
    reduce_sum x4 -> x3, other arithmetic: 29.9 us -> 2.12 us  [the longest x1 0.91 us: shards(): jnp.sum(mlp_block * mlp_block)]
    concatenate x1 -> x5, other arithmetic: 45.3 us -> 18.6 us  [the longest x1 15.6 us: reduce_mlp(): summed = scatter_sum(jnp.concatenate([up_part, grad_down], axis=0))]
  transfers between devices with their start and end apart: 4 -> 11, of which waited for: 4 -> 9; matrix products, arithmetic and copies ran while one was open for 10% -> 28% of each run, Pallas kernels for 0% -> 0%
where the time goes in v1:
time: 644 us; the launch traced here: 635 us
  waiting for transfers between devices  254 us (39%)
  local copies, waits for them, and re-layouts  148 us (23%)
  matrix products  139 us (22%)
  other arithmetic  57.1 us (9%)
  between operations  20.9 us (3%)
  starting transfers between devices  15.4 us (2%)
    dot_general x26, matrix products, product(): return jnp.einsum(form, left, right, preferred_element_type=jnp.float32)  101 us
    all_gather x1, waiting for transfers between devices, gather_weights(): square = lax.all_gather(attn_rows, AXES, axis=0, tiled=True)  72.9 us
    all_gather x1, waiting for transfers between devices, gather_weights(): stack = lax.all_gather(mlp_rows, AXES, axis=0, tiled=True)  70.1 us
    reduce_scatter x2, waiting for transfers between devices, scatter_sum(): return lax.psum_scatter(part, 'fsdp', scatter_dimension=0, tiled=True)  52.3 us
    reduce_scatter x2, waiting for transfers between devices, scatter_sum(): part = lax.psum_scatter(full, 'dp', scatter_dimension=0, tiled=True)  50.9 us
    unnamed x144, local copies, waits for them, and re-layouts  34.9 us
    concatenate x1, other arithmetic, reduce_mlp(): summed = scatter_sum(jnp.concatenate([up_part, grad_down], axis=0))  15.6 us
  transfers between devices with their start and end apart: 11, of which 9 were waited for; matrix products, arithmetic and copies ran while one was open for 28% of the time, Pallas kernels for 0%

profile of v1, /device:TPU:0, one launch (start us, length us, event | category | flops | bytes accessed | tf_op | source)
XLA Modules:
  0.0 635.1 jit_solution(13627777025050797331)
XLA Ops:
  9.3 4.9 collective-permute-start.1
  21.9 4.2 collective-permute-start
  34.1 70.1 %all-gather.5.cloned.1.call-done = bf16[128,48,768]{2,1,0:T(8,128)(2,1)} async-done(((bf16[4,48,768]{2,1,0:T(8,128)(2,1)}), bf16[128,48,768]{2,1,0:T(8,128)(2,1)}) %all-gather.5.cloned.1.call-update) | async-done | bytes 9437200 | tf_op jit(solution)/shard_map/all_gather | solution.py:104
  104.2 6.6 %fusion.100 = (bf16[64,48,768]{2,1,0:T(8,128)(2,1)S(1)}, bf16[64,48,768]{2,1,0:T(8,128)(2,1)}) fusion(bf16[128,48,768]{2,1,0:T(8,128)(2,1)} %all-gather.5.cloned.1.call-done), kind=kLoop, calls=%fused_computation.201 | loop fusion | bytes 18874368 | tf_op jit(solution)/shard_map/slice | solution.py:106
  110.8 2.4 copy.227
  113.3 3.2 copy.283
  116.4 72.9 %all-gather.3.cloned.1.call-done = bf16[768,6400]{1,0:T(8,128)(2,1)} async-done(((bf16[24,6400]{1,0:T(8,128)(2,1)}), bf16[768,6400]{1,0:T(8,128)(2,1)}) %all-gather.3.cloned.1.call-update) | async-done | bytes 9830416 | tf_op jit(solution)/shard_map/all_gather | solution.py:103
  190.3 5.8 convolution_convert_fusion.4
  196.1 4.5 copy.214
  200.6 7.1 %reshape.352 = bf16[8,64,3,12,64]{1,0,4,3,2:T(8,128)(2,1)} reshape(bf16[512,2304]{0,1:T(8,128)(2,1)} %copy.214) | data formatting | bytes 4718592 | tf_op jit(solution)/shard_map/reshape | solution.py:224
  207.7 4.6 fusion.102
  212.3 3.0 copy.273
  215.2 3.0 copy.272
  218.2 2.8 fusion.103
  224.5 2.4 copy.219
  227.0 3.5 convert_element_type.233
  230.4 2.6 fusion.104
  234.2 3.1 convolution_convert_fusion.14
  237.3 3.8 reshape.381
  241.0 4.1 copy.245
  245.2 7.4 %convolution_convert_fusion = bf16[1536,2048]{1,0:T(8,128)(2,1)S(1)} fusion(bf16[2048,768]{1,0:T(8,128)(2,1)S(1)} %copy-done, bf16[768,6400]{1,0:T(8,128)(2,1)} %all-gather.3.cloned.1.call-done), kind=kOutput, calls=%fused_computation.5 | convolution fusion | flops 4834983936 | bytes 11796480 | tf_op jit(solution)/shard_map/dot_general | solution.py:238
  252.6 2.7 copy.282
  256.8 2.4 multiply_reduce_fusion.1
  261.8 3.7 fusion.62
  265.6 2.4 copy.224
  268.0 3.6 convert_element_type.245
  271.6 3.0 fusion.105
  274.9 5.0 fusion.92
  279.9 5.1 convolution_convert_fusion.1
  285.1 9.2 %fusion.3 = bf16[512,3072]{1,0:T(8,128)(2,1)S(1)} fusion(f32[512,3072]{1,0:T(8,128)S(1)} %fusion.92, bf16[3072,768]{1,0:T(8,128)(2,1)S(1)} %bitcast.179, bf16[512,768]{1,0:T(8,128)(2,1)S(1)} %copy-done.27, pred[512]{0:T(512)(128)(4,1)S(1)} %lt.46), kind=kOutput, calls=%fused_computation.9 | convolution fusion | flops 2454061056 | bytes 14942720 | tf_op jit(solution)/shard_map/td,fd->tf/dot_general | solution.py:41
  296.0 4.8 convolution_convert_fusion.2
  300.8 9.8 %reshape.369 = bf16[16,48,4,768]{3,2,1,0:T(4,128)(2,1)} reshape(bf16[768,3072]{1,0:T(8,128)(2,1)} %convolution_convert_fusion.2) | data formatting | bytes 9437184 | tf_op jit(solution)/shard_map/reshape | solution.py:131
  310.6 3.4 copy.252
  314.3 15.6 %pad_maximum_fusion = bf16[6144,768]{1,0:T(8,128)(2,1)} fusion(bf16[3072,768]{1,0:T(8,128)(2,1)S(1)} %bitcast.181, bf16[3072,768]{1,0:T(8,128)(2,1)S(1)} %bitcast.166), kind=kLoop, calls=%fused_computation.2 | loop fusion | flops 18874368 | bytes 18874368 | tf_op jit(solution)/shard_map/concatenate | solution.py:132
  330.0 6.8 %multiply_reduce_fusion.3 = (bf16[768]{0:T(1024)(128)(2,1)S(1)}, f32[512]{0:T(512)S(1)}, bf16[768]{0:T(1024)(128)(2,1)S(1)}, f32[512,768]{1,0:T(8,128)S(1)}) fusion(f32[512,768]{1,0:T(8,128)} %copy-done.8, f32[512]{0:T(512)S(1)} %fusion.85, f32[512]{0:T(512)S(1)} %broadcast_multiply_fusion, f32[768]{0:T(1024)S(1)} %reshape.379, ...), kind=kOutput, calls=%fused_computation.85 | convolution fusion | flops 2419062784 | bytes 11022336 | tf_op jit(solution)/shard_map/tf,df->td/dot_general | solution.py:41
  339.9 3.3 convolution_convert_fusion.13
  343.2 4.0 reshape.382
  347.2 4.1 copy.246
  351.4 8.4 %multiply_reduce_fusion = (f32[8,12,64]{2,1,0:T(8,128)S(1)}, f32[8,12,64,256]{3,2,1,0:T(8,128)S(1)}) fusion(f32[8,12,64,256]{3,2,1,0:T(8,128)} %copy-done.1, f32[8,12,64]{2,1,0:T(8,128)S(1)} %log_add_fusion, bf16[8,64,12,64]{1,3,2,0:T(8,128)(2,1)} %copy.246, bf16[8,256,1,12,64]{1,0,4,3,2:T(8,128)(2,1)} %copy-done.23), kind=kOutput, calls=%fused_computation.15 | convolution fusion | flops 207611904 | bytes 16564224 | tf_op jit(solution)/shard_map/cqhe,ckhe->chqk/dot_general | solution.py:41
  366.0 4.6 copy.247
  370.6 5.4 copy.284
  375.9 2.9 fusion.61
  378.8 2.8 copy.231
  381.6 3.6 reshape.359
  385.3 3.4 multiply_reduce_fusion.4
  392.3 3.0 convolution_convert_fusion.12
  395.3 3.8 reshape.383
  399.1 4.1 copy.241
  403.2 4.2 multiply_reduce_fusion.2
  412.7 2.7 pad_maximum_fusion.2
  415.4 7.0 %copy.244 = bf16[8,64,3,12,64]{1,0,4,3,2:T(8,128)(2,1)} copy(bf16[8,64,3,12,64]{4,1,3,0,2:T(8,128)(2,1)} %pad_maximum_fusion.2) | data formatting | bytes 4718592 | tf_op jit(solution)/shard_map/stack | solution.py:297
  422.4 7.6 %convert_element_type.264 = bf16[512,2304]{0,1:T(8,128)(2,1)} reshape(bf16[8,64,3,12,64]{1,0,4,3,2:T(8,128)(2,1)} %copy.244) | data formatting | bytes 4718592 | tf_op jit(solution)/shard_map/convert_element_type | solution.py:298
  430.0 5.2 fusion.93
  436.6 6.2 fusion.7
  446.9 9.3 %fusion.19 = bf16[768,6400]{1,0:T(8,128)(2,1)} fusion(bf16[768,6400]{1,0:T(8,128)(2,1)} %fusion.49, bf16[2048,1536]{0,1:T(8,128)(2,1)} %bitcast.167, bf16[2048,768]{1,0:T(8,128)(2,1)S(1)} %copy-done), kind=kOutput, calls=%fused_computation.52 | convolution fusion | flops 4833017856 | bytes 11796480 | tf_op jit(solution)/shard_map/td,tf->df/dot_general | solution.py:41
  460.8 4.4 add_convert_fusion
  465.2 11.3 %add_convert_fusion.1 = bf16[512,768]{1,0:T(8,128)(2,1)} fusion(f32[512,768]{1,0:T(8,128)S(1)} %copy-done.10, bf16[3072,768]{1,0:T(8,128)(2,1)} %bitcast.176, f32[512,3072]{1,0:T(8,128)} %copy-done.59), kind=kOutput, calls=%fused_computation.93 | convolution fusion | flops 2430861312 | bytes 13369344 | tf_op jit(solution)/shard_map/dot_general | solution.py:249
  476.5 8.2 %convolution_convert_fusion.6 = bf16[2048,768]{1,0:T(8,128)(2,1)} fusion(bf16[2048,1536]{0,1:T(8,128)(2,1)S(1)} %bitcast.170, bf16[768,6400]{1,0:T(8,128)(2,1)} %all-gather.3.cloned.1.call-done), kind=kOutput, calls=%fused_computation.30 | convolution fusion | flops 4833411072 | bytes 11796480 | tf_op jit(solution)/shard_map/tf,df->td/dot_general | solution.py:41
  484.7 50.9 %reduce-scatter.5.cloned.1.call-done = bf16[96,6400]{1,0:T(8,128)(2,1)} async-done(((bf16[768,6400]{1,0:T(8,128)(2,1)}), bf16[96,6400]{1,0:T(8,128)(2,1)}) %reduce-scatter.5.cloned.1.call-update) | async-done | bytes 1228816 | tf_op jit(solution)/shard_map/reduce_scatter | solution.py:123
  535.7 31.5 %reduce-scatter.11.cloned.1.call-done = bf16[192,768]{1,0:T(8,128)(2,1)} async-done(((bf16[768,768]{1,0:T(8,128)(2,1)}), bf16[192,768]{1,0:T(8,128)(2,1)}) %reduce-scatter.11.cloned.1.call-update) | async-done | bytes 294928 | tf_op jit(solution)/shard_map/reduce_scatter | solution.py:124
  577.6 20.8 %reduce-scatter.7.cloned.1.call-done = bf16[24,6400]{1,0:T(8,128)(2,1)} async-done(((bf16[96,6400]{1,0:T(8,128)(2,1)}), bf16[24,6400]{1,0:T(8,128)(2,1)}) %reduce-scatter.7.cloned.1.call-update) | async-done | bytes 307216 | tf_op jit(solution)/shard_map/reduce_scatter | solution.py:124
  606.8 3.2 all-to-all-start
  612.0 3.6 collective-permute-done.2
  618.5 3.9 fusion.96
  (259 shorter events, 81.2 us)
Async XLA Ops:
  7.2 238.0 %copy-start = (bf16[2048,768]{1,0:T(8,128)(2,1)S(1)}, bf16[2048,768]{1,0:T(8,128)(2,1)}, u32[]{:S(2)}) copy-start(bf16[2048,768]{1,0:T(8,128)(2,1)} %param.15) | copy-start | bytes 9437188
  7.2 97.0 %all-gather.5.cloned.1.call-start = ((), (), s32[]{:S(2)}) async-start(), calls=%async_computation.6 | async-start | bytes 9732096 | tf_op jit(solution)/shard_map/all_gather | solution.py:104
  9.3 6.3 collective-permute-start.1
  16.8 13.5 %copy-start.58 = (s32[8]{0:T(128)S(1)}, s32[8]{0:T(128)}, u32[]{:S(2)}) copy-start(s32[8]{0:T(128)} %param.17) | copy-start | bytes 100
  20.6 168.7 %all-gather.3.cloned.1.call-start = ((), (), s32[]{:S(2)}) async-start(), calls=%async_computation.5 | async-start | bytes 10137600 | tf_op jit(solution)/shard_map/all_gather | solution.py:103
  21.9 5.5 collective-permute-start
  30.2 430.2 %reduce-scatter.9.cloned.1.call-start = ((), (), s32[]{:S(2)}) async-start(), calls=%async_computation.9 | async-start | bytes 10616832 | tf_op jit(solution)/shard_map/reduce_scatter | solution.py:123
  31.8 158.4 %copy-start.48 = (f32[512]{0:T(512)}, f32[512]{0:T(512)S(1)}, u32[]{:S(2)}) copy-start(f32[512]{0:T(512)S(1)} %broadcast_multiply_fusion.2) | copy-start | bytes 6148
  33.9 156.3 %copy-start.52 = (f32[512]{0:T(512)}, f32[512]{0:T(512)S(1)}, u32[]{:S(2)}) copy-start(f32[512]{0:T(512)S(1)} %fusion.83) | copy-start | bytes 6148
  190.2 5.9 copy-start.46
  190.2 43.2 %copy-start.54 = (f32[768]{0:T(1024)}, f32[768]{0:T(1024)S(1)}, u32[]{:S(2)}) copy-start(f32[768]{0:T(1024)S(1)} %reshape.378) | copy-start | bytes 9220
  190.3 5.8 copy-start.56
  221.1 3.5 copy-start.2
  221.1 2.5 copy-start.24
  255.9 3.3 copy-start.20
  255.9 5.3 copy-start.23
  259.2 2.6 copy-start.1
  274.6 19.8 %copy-start.8 = (f32[512,768]{1,0:T(8,128)}, f32[512,768]{1,0:T(8,128)S(1)}, u32[]{:S(2)}) copy-start(f32[512,768]{1,0:T(8,128)S(1)} %get-tuple-element.58) | copy-start | bytes 4718596
  274.9 5.0 copy-start.27
  274.9 10.1 %slice-start.4 = ((s8[4718592]{0:T(1024)(128)(4,1)}), s8[4194304]{0:T(1024)(128)(4,1)S(1)}, s32[]{:S(2)}) async-start(s8[4718592]{0:T(1024)(128)(4,1)} %bitcast.177), calls=%async_computation.15 | async-start | bytes 8388608
  279.9 5.1 copy-start.59
  279.9 5.1 slice-start.5
  310.6 3.6 slice-start.6
  310.6 3.7 slice-start.7
  330.0 205.7 %reduce-scatter.5.cloned.1.call-start = ((), (), s32[]{:S(2)}) async-start(), calls=%async_computation.7 | async-start | bytes 11059200 | tf_op jit(solution)/shard_map/reduce_scatter | solution.py:123
  330.0 6.8 %copy-start.9 = (f32[512,768]{1,0:T(8,128)S(1)}, f32[512,768]{1,0:T(8,128)}, u32[]{:S(2)}) copy-start(f32[512,768]{1,0:T(8,128)} %copy-done.8) | copy-start | bytes 4718596
  336.8 1.9 copy-start.28
  351.3 8.4 %slice-start = ((s8[6291456]{0:T(1024)(128)(4,1)}), s8[4194304]{0:T(1024)(128)(4,1)S(1)}, s32[]{:S(2)}) async-start(s8[6291456]{0:T(1024)(128)(4,1)} %bitcast.159), calls=%async_computation.11 | async-start | bytes 8388608
  351.4 8.4 %slice-start.1 = ((s8[6291456]{0:T(1024)(128)(4,1)}), s8[2097152]{0:T(1024)(128)(4,1)S(1)}, s32[]{:S(2)}) async-start(s8[6291456]{0:T(1024)(128)(4,1)} %bitcast.159), calls=%async_computation.12 | async-start | bytes 4194304
  359.8 2.1 copy-start.19
  370.6 5.4 copy-start.21
  385.2 3.5 copy-start.12
  388.7 1.9 copy-start.17
  388.7 2.1 copy-start.29
  403.2 4.2 copy-start.3
  422.4 7.6 %copy-start.47 = (f32[768]{0:T(1024)S(1)}, f32[768]{0:T(1024)}, u32[]{:S(2)}) copy-start(f32[768]{0:T(1024)} %copy-done.46) | copy-start | bytes 9220
  422.4 7.6 %copy-start.49 = (f32[512]{0:T(512)S(1)}, f32[512]{0:T(512)}, u32[]{:S(2)}) copy-start(f32[512]{0:T(512)} %copy-done.48) | copy-start | bytes 6148
  430.0 5.3 copy-start.51
  430.0 5.3 copy-start.22
  430.0 5.3 copy-start.53
  430.0 6.6 %copy-start.57 = (f32[768]{0:T(1024)S(1)}, f32[768]{0:T(1024)}, u32[]{:S(2)}) copy-start(f32[768]{0:T(1024)} %copy-done.56) | copy-start | bytes 9220
  436.6 6.2 copy-start.6
  436.6 6.2 copy-start.30
  442.9 1.9 copy-start.13
  442.9 1.9 copy-start.41
  442.9 1.9 copy-start.55
  446.9 9.3 %copy-start.31 = (bf16[512,768]{0,1:T(8,128)(2,1)S(1)}, bf16[512,768]{0,1:T(8,128)(2,1)}, u32[]{:S(2)}) copy-start(bf16[512,768]{0,1:T(8,128)(2,1)} %convert_element_type.245) | copy-start | bytes 2359300
  446.9 9.3 %copy-start.40 = (bf16[512,768]{1,0:T(8,128)(2,1)S(1)}, bf16[512,768]{1,0:T(8,128)(2,1)}, u32[]{:S(2)}) copy-start(bf16[512,768]{1,0:T(8,128)(2,1)} %copy-done.39) | copy-start | bytes 2359300
  458.9 108.2 %reduce-scatter.11.cloned.1.call-start = ((), (), s32[]{:S(2)}) async-start(), calls=%async_computation.10 | async-start | bytes 1474560 | tf_op jit(solution)/shard_map/reduce_scatter | solution.py:124
  460.4 137.9 %reduce-scatter.7.cloned.1.call-start = ((), (), s32[]{:S(2)}) async-start(), calls=%async_computation.8 | async-start | bytes 1536000 | tf_op jit(solution)/shard_map/reduce_scatter | solution.py:124
  460.7 4.5 copy-start.10
  460.8 15.8 %slice-start.2 = ((s8[6291456]{0:T(1024)(128)(4,1)}), s8[4194304]{0:T(1024)(128)(4,1)S(1)}, s32[]{:S(2)}) async-start(s8[6291456]{0:T(1024)(128)(4,1)} %bitcast.168), calls=%async_computation.13 | async-start | bytes 8388608
  465.2 11.3 %slice-start.3 = ((s8[6291456]{0:T(1024)(128)(4,1)}), s8[2097152]{0:T(1024)(128)(4,1)S(1)}, s32[]{:S(2)}) async-start(s8[6291456]{0:T(1024)(128)(4,1)} %bitcast.168), calls=%async_computation.14 | async-start | bytes 4194304
  567.1 8.8 %copy-start.26 = (bf16[192,768]{1,0:T(8,128)(2,1)S(1)}, bf16[192,768]{1,0:T(8,128)(2,1)}, u32[]{:S(2)}) copy-start(bf16[192,768]{1,0:T(8,128)(2,1)} %reduce-scatter.11.cloned.1.call-done) | copy-start | bytes 884740
  574.6 36.7 %collective-permute-start.3 = (f32[1536]{0:T(1024)S(1)}, f32[1536]{0:T(1024)S(1)}, u32[]{:S(2)}, u32[]{:S(2)}) collective-permute-start(f32[1536]{0:T(1024)S(1)} %slice.176), channel_id=1, source_target_pairs={{1,0},{2,1},{3,2},{4,3},{5,4},{6,5},{7,6},{8,7},{9,8},{10,9},{11,1... | collective-permute-start | bytes 18440 | tf_op jit(solution)/shard_map/ppermute | solution.py:80
  606.8 10.4 %all-to-all-start = ((f32[32,1,128]{2,1,0:T(1,128)}), f32[32,1,128]{2,1,0:T(1,128)S(1)}, u32[]{:S(2)}, u32[]{:S(2)}) async-start(f32[32,1,128]{2,1,0:T(1,128)} %broadcast_in_dim.55), calls=%async_computation.4 | async-start | bytes 32768 | tf_op jit(solution)/shard_map/all_to_all | solution.py:153
  610.0 5.6 collective-permute-start.2
  618.5 4.0 copy-start.42
  618.5 4.9 copy-start.34
  618.5 4.9 copy-start.35
  618.5 4.9 copy-start.44
  618.5 4.9 copy-start.45
  622.4 4.3 copy-start.36
  622.4 3.2 copy-start.43
  (16 other events, 18.4 us)
Sparse Core Ops, SparseCore 0:
  20.7 83.4 all-gather.4
  107.6 81.6 all-gather.2
  330.1 75.3 reduce-scatter.8
  459.1 76.5 reduce-scatter.4
  537.8 29.2 reduce-scatter.10
  569.3 29.0 reduce-scatter.6
